TPU v7x, 512 devices: a whole 4x8x8 slice. The times are simulated.
512 devices in a mesh: item: 8 (over y), rows: 32 (over z, x_hi, core), hid: 2 (over x_lo).
Axes of the slice: x: 4 (x_hi: 2, x_lo: 2; x = x_hi * 2 + x_lo), y: 8, z: 8, core: 2. Of those that a mesh axis runs over, the one named last changes fastest.
Arguments:
- latents: float32 [16, 32, 2048], P('item', 'rows'), may hold values from -6 to 6
- heights: int32 [16], P('item'), may hold values from 8 to 32, as said below
- widths: int32 [16], P('item'), may hold values from 8 to 32, as said below
- slot_item: int32 [16], P('item'), may hold values from 0 to 15, each once
- step_index: int32 [1], replicated, may hold values from 0 to 27
- cond_table: float32 [16, 5, 1536], replicated, may hold values from -9 to 9
- text_kv: bfloat16 [16, 2, 154, 768], P('item', None, None, 'hid'), may hold values from -175 to 175
- patch_weight: bfloat16 [64, 1536], replicated, may hold values from -0.75 to 0.75
- qkv_weight: bfloat16 [3, 1536, 768], P(None, ('item', 'rows'), 'hid'), may hold values from -0.15625 to 0.15625
- out_weight: bfloat16 [768, 1536], P('hid', ('item', 'rows')), may hold values from -0.21875 to 0.21875
- final_weight: bfloat16 [1536, 64], replicated, may hold values from -0.15625 to 0.15625
Outputs:
- next_latents: float32 [16, 32, 2048], P('item', 'rows')
- denoised: float32 [16, 32, 2048], P('item', 'rows')
Inputs may be any that keep to these rules, and one draw needn't show every extreme that they name: `heights`: every grid has at least 8 rows, and some item has exactly 32. `widths`: every grid has at least 8 columns, and some item has exactly 32. `slot_item`: each request is served by exactly one slot.
All inputs are finite; a program needn't handle non-finite values.
Results may differ from a plain program's by a relative error of at most 0.007.
Values may be sent and summed in bfloat16 or wider, within the bound.
A program may use at most 64 MiB of HBM per device.

v0:
```python
import jax
import jax.numpy as jnp
from jax import lax
from jax.sharding import PartitionSpec as P

HD = 64
STEPS = 28


def sigma_level(position):
    fraction = 1.0 - position / STEPS
    return 3.0 * fraction / (1.0 + 2.0 * fraction)


def position_embed(row_pos, col_count, model_width):
    quarter = model_width // 4
    frequency = 1.0 / 10000.0 ** (jnp.arange(quarter, dtype=jnp.float32) / quarter)
    col_pos = jnp.arange(col_count, dtype=jnp.float32)
    row_angle = row_pos[:, None] * frequency[None, :]
    col_angle = col_pos[:, None] * frequency[None, :]
    row_part = jnp.concatenate([jnp.sin(row_angle), jnp.cos(row_angle)], 1)
    col_part = jnp.concatenate([jnp.sin(col_angle), jnp.cos(col_angle)], 1)
    row_full = jnp.broadcast_to(
        row_part[:, None, :], (row_pos.shape[0], col_count, model_width // 2)
    )
    col_full = col_part[None, :, :]
    return jnp.concatenate([row_full, col_full], 2)


def normalize(values):
    mean_rows = jnp.mean(values, -1, keepdims=True)
    centered = values - mean_rows
    return centered * lax.rsqrt(jnp.mean(centered * centered, -1, keepdims=True) + 1e-06)


def body(
    latents,
    heights,
    widths,
    slot_item,
    step_index,
    cond_table,
    text_kv,
    patch_weight,
    qkv_weight,
    out_weight,
    final_weight,
):
    slot_count = latents.shape[0]
    rows_here = latents.shape[1]
    channels = patch_weight.shape[0]
    model_width = patch_weight.shape[1]
    col_count = latents.shape[2] // channels
    local_width = text_kv.shape[3]
    heads_here = local_width // HD
    text_count = text_kv.shape[2]
    per_slot = rows_here * col_count
    tok_rows = slot_count * per_slot
    row_start = lax.axis_index("rows") * rows_here
    row_pos = (row_start + jnp.arange(rows_here, dtype=jnp.int32)).astype(jnp.float32)
    patches = latents.reshape(tok_rows, channels).astype(jnp.bfloat16)
    embedded = jnp.dot(patches, patch_weight, preferred_element_type=jnp.float32).reshape(
        slot_count, per_slot, model_width
    )
    embedded = embedded + position_embed(row_pos, col_count, model_width)
    entries = cond_table.shape[0]
    chosen = (slot_item[:, None] == jnp.arange(entries, dtype=jnp.int32)[None, :]).astype(
        jnp.float32
    )
    conditions = jnp.dot(
        chosen, cond_table.reshape(entries, 5 * model_width), precision=lax.Precision.HIGHEST
    )
    conditions = conditions.reshape(slot_count, 5, model_width)
    normed = (normalize(embedded) * (1.0 + conditions[:, 1:2, :]) + conditions[:, 0:1, :]).astype(
        jnp.bfloat16
    )
    flat_rows = normed.reshape(tok_rows, model_width)
    projected = jnp.einsum(
        "td,kdh->kth",
        flat_rows,
        lax.all_gather(qkv_weight, ("item", "rows"), axis=1, tiled=True),
        preferred_element_type=jnp.float32,
    )
    projected = projected.astype(jnp.bfloat16)
    queries = projected[0].reshape(slot_count, per_slot, heads_here, HD)
    image_kv = projected[1:].reshape(2, slot_count, rows_here, col_count, local_width)
    score_scale = HD ** (-0.5)
    text_keys = text_kv[:, 0].reshape(slot_count, text_count, heads_here, HD)
    text_vals = text_kv[:, 1].reshape(slot_count, text_count, heads_here, HD)
    text_score = (
        jnp.einsum("sqhd,skhd->shqk", queries, text_keys, preferred_element_type=jnp.float32)
        * score_scale
    )
    first_top = jnp.max(text_score, -1)
    text_weights = jnp.exp(text_score - first_top[..., None])
    first_total = jnp.sum(text_weights, -1)
    first_acc = jnp.einsum(
        "shqk,skhd->shqd",
        text_weights.astype(jnp.bfloat16),
        text_vals,
        preferred_element_type=jnp.float32,
    )
    col_live = jnp.arange(col_count, dtype=jnp.int32)[None, :] < widths[:, None]
    gathered = lax.all_gather(image_kv, "rows", axis=2, tiled=True)
    run_top = first_top
    run_total = first_total
    run_acc = first_acc
    key_rows = gathered.shape[2]
    key_piece = gathered[0].reshape(slot_count, key_rows * col_count, heads_here, HD)
    val_piece = gathered[1].reshape(slot_count, key_rows * col_count, heads_here, HD)
    scores = (
        jnp.einsum("sqhd,skhd->shqk", queries, key_piece, preferred_element_type=jnp.float32)
        * score_scale
    )
    key_index = jnp.arange(key_rows, dtype=jnp.int32)
    live_mask = (key_index[None, :, None] < heights[:, None, None]) & col_live[:, None, :]
    live_mask = live_mask.reshape(slot_count, 1, 1, key_rows * col_count)
    scores = jnp.where(live_mask, scores, -1e30)
    new_top = jnp.maximum(run_top, jnp.max(scores, -1))
    factor = jnp.exp(run_top - new_top)
    weights = jnp.exp(scores - new_top[..., None])
    run_total = run_total * factor + jnp.sum(weights, -1)
    run_acc = run_acc * factor[..., None] + jnp.einsum(
        "shqk,skhd->shqd",
        weights.astype(jnp.bfloat16),
        val_piece,
        preferred_element_type=jnp.float32,
    )
    run_top, run_total, run_acc = (new_top, run_total, run_acc)
    attended = (
        (run_acc / run_total[..., None])
        .transpose(0, 2, 1, 3)
        .reshape(tok_rows, local_width)
        .astype(jnp.bfloat16)
    )
    partial_value = jnp.dot(
        attended,
        lax.all_gather(out_weight, ("item", "rows"), axis=1, tiled=True),
        preferred_element_type=jnp.float32,
    )
    summed = lax.psum(partial_value.astype(jnp.bfloat16), "hid").astype(jnp.float32)
    summed = summed.reshape(slot_count, per_slot, model_width)
    residual = embedded + conditions[:, 2:3, :] * summed
    final_in = (normalize(residual) * (1.0 + conditions[:, 4:5, :]) + conditions[:, 3:4, :]).astype(
        jnp.bfloat16
    )
    velocity = jnp.dot(
        final_in.reshape(tok_rows, model_width), final_weight, preferred_element_type=jnp.float32
    )
    position = step_index[0].astype(jnp.float32)
    sigma_now = sigma_level(position)
    sigma_next = sigma_level(position + 1.0)
    row_global = row_start + jnp.arange(rows_here, dtype=jnp.int32)
    live_patch = (row_global[None, :, None] < heights[:, None, None]) & col_live[:, None, :]
    velocity = velocity.reshape(slot_count, rows_here, col_count, channels)
    live_velocity = jnp.where(live_patch[..., None], velocity, 0.0).reshape(
        slot_count, rows_here, col_count * channels
    )
    next_latents = latents + (sigma_next - sigma_now) * live_velocity
    denoised = latents - sigma_now * live_velocity
    return (next_latents, denoised)


def solution(mesh):
    return jax.shard_map(
        body,
        mesh=mesh,
        in_specs=(
            P("item", "rows", None),
            P("item"),
            P("item"),
            P("item"),
            P(),
            P(),
            P("item", None, None, "hid"),
            P(),
            P(None, ("item", "rows"), "hid"),
            P("hid", ("item", "rows")),
            P(),
        ),
        out_specs=(P("item", "rows", None), P("item", "rows", None)),
        check_vma=False,
    )
```

profile of v0, /device:TPU:1, one launch (start us, length us, event | category | flops | bytes accessed | tf_op | source)
XLA Modules:
  0.0 422.9 jit_solution(1402297968687768749)
XLA Ops:
  7.2 0.0 all-gather.5.cloned.1.call-start
  7.2 1.4 copy.35
  8.6 0.0 all-gather.5.cloned.1.call-update
  8.6 0.0 all-gather.9.cloned.1.call-start
  8.7 0.7 all-gather.9.cloned.1.call-update
  9.4 0.0 all-gather.7.cloned.1.call-start
  9.5 0.1 fusion.49
  9.5 0.2 fusion.42
  9.8 0.8 convert_reduce_fusion
  10.6 0.1 convert_element_type.46
  10.7 1.2 fusion.56
  11.9 0.2 multiply_reduce_fusion.1
  12.1 0.3 fusion.25
  12.4 0.1 add_convert_fusion.1
  12.6 136.8 %all-gather.5.cloned.1.call-done = bf16[3,1536,384]{2,0,1:T(4,128)(2,1)} async-done(((bf16[3,6,384]{2,0,1:T(4,128)(2,1)}), bf16[3,1536,384]{2,0,1:T(4,128)(2,1)}) %all-gather.5.cloned.1.call-update) | async-done | bytes 3538960 | tf_op jit(solution)/shard_map/all_gather | solution.py:81
  149.4 3.1 fusion.20
  152.5 0.6 slice.48
  153.1 0.0 all-gather.7.cloned.1.call-update
  153.2 0.0 all-reduce.2.cloned.1.call-start
  153.2 0.1 broadcast_and_fusion.1
  153.3 0.1 broadcast_and_fusion
  153.4 0.1 and.40
  153.5 0.7 fusion.54
  154.2 0.5 copy.37
  154.7 0.5 copy.39
  155.2 109.8 %all-gather.9.cloned.1.call-done = bf16[256,6,384]{2,1,0:T(8,128)(2,1)} async-done(((bf16[1,6,384]{2,1,0:T(8,128)(2,1)}), bf16[256,6,384]{2,1,0:T(8,128)(2,1)}) %all-gather.9.cloned.1.call-update) | async-done | bytes 1179664 | tf_op jit(solution)/shard_map/all_gather | solution.py:138
  265.0 3.3 reshape.279
  268.3 0.1 reshape_squeeze.15
  268.4 0.3 fusion.57
  268.7 0.2 fusion.28
  268.9 85.4 %all-gather.7.cloned.1.call-done = bf16[2,2,32,32,384]{4,3,2,1,0:T(8,128)(2,1)} async-done(((bf16[2,2,1,32,384]{4,3,2,1,0:T(8,128)(2,1)}), bf16[2,2,32,32,384]{4,3,2,1,0:T(8,128)(2,1)}) %all-gather.7.cloned.1.call-update) | async-done | bytes 3145744 | tf_op jit(solution)/shard_map/all_gather | solution.py:104
  354.4 3.5 fusion.53
  357.8 3.7 reshape_squeeze.18
  361.6 3.4 fusion.58
  365.0 5.9 %reshape_squeeze.19 = bf16[2,1024,6,64]{3,2,1,0:T(8,128)(2,1)} reshape(bf16[1,2,32,32,384]{4,3,2,1,0:T(8,128)(2,1)} %get-tuple-element.5) | data formatting | bytes 3145728 | tf_op jit(solution)/shard_map/reshape;squeeze | solution.py:110
  370.9 0.4 fusion.8
  371.3 3.3 fusion.16
  374.6 0.3 fusion.19
  375.0 0.1 convert_element_type.54
  375.1 0.7 copy-done.1
  375.9 1.2 convolution_convert_fusion
  377.8 34.3 %all-reduce.2.cloned.1.call-done = bf16[2,32,1536]{2,1,0:T(8,128)(2,1)} async-done(((bf16[2,32,1536]{2,1,0:T(8,128)(2,1)}), bf16[2,32,1536]{2,1,0:T(8,128)(2,1)}) %all-reduce.2.cloned.1.call-update) | async-done | bytes 196624 | tf_op jit(solution)/shard_map/psum | solution.py:141
  412.1 1.1 fusion.38
  413.2 1.1 multiply_reduce_fusion
  414.3 1.2 broadcast_multiply_fusion
  415.5 0.1 mul.213
  415.6 0.1 mul.214
  415.7 0.6 fusion.55
  (31 shorter events, 0.2 us)
Async XLA Ops:
  7.2 4.9 %copy-start = (f32[16,5,1536]{2,0,1:T(8,128)S(1)}, f32[16,5,1536]{2,0,1:T(8,128)}, u32[]{:S(2)}) copy-start(f32[16,5,1536]{2,0,1:T(8,128)} %param.16) | copy-start | bytes 1474564
  7.2 4.9 %copy-start.4 = (s32[2]{0:T(128)S(1)}, s32[2]{0:T(128)}, u32[]{:S(2)}) copy-start(s32[2]{0:T(128)} %param.14) | copy-start | bytes 28
  7.2 142.2 %all-gather.5.cloned.1.call-start = ((), (), s32[]{:S(2)}) async-start(), calls=%async_computation | async-start | bytes 4737024 | tf_op jit(solution)/shard_map/all_gather | solution.py:81
  8.6 256.3 %all-gather.9.cloned.1.call-start = ((), (), s32[]{:S(2)}) async-start(), calls=%async_computation.3 | async-start | bytes 1579008 | tf_op jit(solution)/shard_map/all_gather | solution.py:138
  9.4 345.0 %all-gather.7.cloned.1.call-start = ((), (), s32[]{:S(2)}) async-start(), calls=%async_computation.1 | async-start | bytes 3244032 | tf_op jit(solution)/shard_map/all_gather | solution.py:104
  149.4 3.9 copy-start.5
  149.4 3.9 copy-start.6
  149.4 4.1 copy-start.2
  153.2 258.9 %all-reduce.2.cloned.1.call-start = ((), (), s32[]{:S(2)}) async-start(), calls=%async_computation.2 | async-start | bytes 393216 | tf_op jit(solution)/shard_map/psum | solution.py:141
  374.6 1.3 copy-start.1
  375.0 39.3 %copy-start.7 = (bf16[1536,64]{0,1:T(8,128)(2,1)S(1)}, bf16[1536,64]{0,1:T(8,128)(2,1)}, u32[]{:S(2)}) copy-start(bf16[1536,64]{0,1:T(8,128)(2,1)} %param.21) | copy-start | bytes 589828
  377.0 38.7 %copy-start.3 = (f32[2,1,2048]{2,1,0:T(1,128)S(1)}, f32[2,1,2048]{2,1,0:T(1,128)}, u32[]{:S(2)}) copy-start(f32[2,1,2048]{2,1,0:T(1,128)} %param.11) | copy-start | bytes 49156
Sparse Core Ops, SparseCore 0:
  12.5 136.7 all-gather.4
  153.5 111.3 all-gather.8
  268.3 86.0 all-gather.6
  377.2 34.8 all-reduce.1
where the time goes:
time: 423 us
  waiting for transfers between devices  367 us (87%)
  local copies, waits for them, and re-layouts  21.5 us (5%)
  between operations  14.8 us (3%)
  matrix products  14.3 us (3%)
  other arithmetic  5.08 us (1%)
    all_gather x1, waiting for transfers between devices, body(): lax.all_gather(qkv_weight, ('item', 'rows'), axis=1, tiled=True)  137 us
    all_gather x1, waiting for transfers between devices, body(): lax.all_gather(out_weight, ('item', 'rows'), axis=1, tiled=True)  110 us
    all_gather x1, waiting for transfers between devices, body(): gathered = lax.all_gather(image_kv, 'rows', axis=2, tiled=True)  85.4 us
    psum x1, waiting for transfers between devices, body(): lax.psum(partial_value.astype(jnp.bfloat16), 'hid').astype(jnp.float32)  34.3 us
  transfers between devices with their start and end apart: 4, of which 4 were waited for; matrix products, arithmetic and copies ran while one was open for 3% of the time, Pallas kernels for 0%

commit v1 on v0

--- a/solution.py
+++ b/solution.py
@@ -135,7 +135,12 @@
     )
     partial_value = jnp.dot(
         attended,
-        lax.all_gather(out_weight, ("item", "rows"), axis=1, tiled=True),
+        jnp.concatenate(
+            lax.all_to_all(
+                jnp.stack([out_weight] * lax.axis_size(("item", "rows"))), ("item", "rows"), 0, 0
+            ),
+            axis=1,
+        ),
         preferred_element_type=jnp.float32,
     )
     summed = lax.psum(partial_value.astype(jnp.bfloat16), "hid").astype(jnp.float32)

time: 423 us -> 337 us (0.80)
  waiting for transfers between devices: 367 us -> 265 us
  starting transfers between devices: 0.16 us -> 11.4 us
    all_gather x1 -> x0, waiting for transfers between devices: 110 us -> none  [body(): lax.all_gather(out_weight, ('item', 'rows'), axis=1, tiled=True)]
    all_to_all x0 -> x1, waiting for transfers between devices: none -> 37.9 us  [body(): lax.all_to_all(jnp.stack([out_weight] * lax.axis_size(('item', 'rows'))),...]
    all_gather x1, waiting for transfers between devices: 85.4 us -> 56.1 us  [body(): gathered = lax.all_gather(image_kv, 'rows', axis=2, tiled=True)]
    all_to_all x0 -> x1, starting transfers between devices: none -> 11.1 us  [body(): lax.all_to_all(jnp.stack([out_weight] * lax.axis_size(('item', 'rows'))),...]
  transfers between devices with their start and end apart: 4 -> 4, of which waited for: 4 -> 4; matrix products, arithmetic and copies ran while one was open for 3% -> 4% of each run, Pallas kernels for 0% -> 0%
where the time goes in v1:
time: 337 us; the launch traced here: 336 us
  waiting for transfers between devices  265 us (79%)
  local copies, waits for them, and re-layouts  24.3 us (7%)
  between operations  14.8 us (4%)
  matrix products  14.3 us (4%)
  starting transfers between devices  11.4 us (3%)
  other arithmetic  6.17 us (2%)
    all_gather x1, waiting for transfers between devices, body(): lax.all_gather(qkv_weight, ('item', 'rows'), axis=1, tiled=True)  137 us
    all_gather x1, waiting for transfers between devices, body(): gathered = lax.all_gather(image_kv, 'rows', axis=2, tiled=True)  56.1 us
    all_to_all x1, waiting for transfers between devices, body(): lax.all_to_all(jnp.stack([out_weight] * lax.axis_size(('item', 'rows'))),...  37.9 us
    psum x1, waiting for transfers between devices, body(): lax.psum(partial_value.astype(jnp.bfloat16), 'hid').astype(jnp.float32)  34.3 us
    all_to_all x1, starting transfers between devices, body(): lax.all_to_all(jnp.stack([out_weight] * lax.axis_size(('item', 'rows'))),...  11.1 us
  transfers between devices with their start and end apart: 4, of which 4 were waited for; matrix products, arithmetic and copies ran while one was open for 4% of the time, Pallas kernels for 0%

profile of v1, /device:TPU:1, one launch (start us, length us, event | category | flops | bytes accessed | tf_op | source)
XLA Modules:
  0.0 336.4 jit_solution(720831609192284192)
XLA Ops:
  7.2 0.0 all-gather.3.cloned.1.call-start
  7.2 1.4 copy.36
  8.6 0.0 all-gather.3.cloned.1.call-update
  8.6 0.0 all-gather.5.cloned.1.call-start
  8.7 0.8 convert_reduce_fusion
  9.5 0.1 convert_element_type.46
  9.6 0.1 fusion.49
  9.7 0.2 fusion.42
  9.9 1.2 fusion.56
  11.1 0.2 multiply_reduce_fusion.1
  11.4 0.3 fusion.25
  11.7 0.6 slice_bitcast_fusion.2
  12.3 0.1 add_convert_fusion.1
  12.4 136.9 %all-gather.3.cloned.1.call-done = bf16[3,1536,384]{2,0,1:T(4,128)(2,1)} async-done(((bf16[3,6,384]{2,0,1:T(4,128)(2,1)}), bf16[3,1536,384]{2,0,1:T(4,128)(2,1)}) %all-gather.3.cloned.1.call-update) | async-done | bytes 3538960 | tf_op jit(solution)/shard_map/all_gather | solution.py:81
  149.4 3.1 fusion.20
  152.4 0.6 slice.48
  153.1 1.3 stack.2
  154.4 11.1 %all-to-all-start = ((bf16[256,384,6]{1,2,0:T(8,128)(2,1)}), bf16[256,384,6]{1,2,0:T(8,128)(2,1)S(1)}, u32[]{:S(2)}, u32[]{:S(2)}) async-start(bf16[256,384,6]{1,2,0:T(8,128)(2,1)} %stack.2), calls=%async_computation | async-start | bytes 3145728 | tf_op jit(solution)/shard_map/all_to_all | solution.py:139
  165.6 0.2 all-reduce.2.cloned.1.call-start
  165.8 0.6 broadcast_and_fusion.1
  166.4 0.1 broadcast_and_fusion
  166.5 0.7 and.40
  167.2 1.5 fusion.54
  168.6 2.0 copy.38
  170.6 1.2 copy.40
  171.8 37.9 %all-to-all-done = bf16[256,384,6]{1,2,0:T(8,128)(2,1)S(1)} async-done(((bf16[256,384,6]{1,2,0:T(8,128)(2,1)}), bf16[256,384,6]{1,2,0:T(8,128)(2,1)S(1)}, u32[]{:S(2)}, u32[]{:S(2)}) %all-to-all-start) | async-done | bytes 1179680 | tf_op jit(solution)/shard_map/all_to_all | solution.py:139
  209.7 1.2 reshape.275
  211.0 0.1 reshape_squeeze.15
  211.1 0.3 fusion.57
  211.4 0.2 fusion.28
  211.6 56.1 %all-gather.5.cloned.1.call-done = bf16[2,2,32,32,384]{4,3,2,1,0:T(8,128)(2,1)} async-done(((bf16[2,2,1,32,384]{4,3,2,1,0:T(8,128)(2,1)}), bf16[2,2,32,32,384]{4,3,2,1,0:T(8,128)(2,1)}) %all-gather.5.cloned.1.call-update) | async-done | bytes 3145744 | tf_op jit(solution)/shard_map/all_gather | solution.py:104
  267.8 3.5 %fusion.53 = (bf16[1,2,32,32,384]{4,3,2,1,0:T(8,128)(2,1)S(1)}, bf16[1,2,32,32,384]{4,3,2,1,0:T(8,128)(2,1)}) fusion(bf16[2,2,32,32,384]{4,3,2,1,0:T(8,128)(2,1)} %all-gather.5.cloned.1.call-done), kind=kLoop, calls=%fused_computation.81 | loop fusion | bytes 6291456 | tf_op jit(solution)/shard_map/slice | solution.py:109
  271.3 3.7 %reshape_squeeze.18 = bf16[2,1024,6,64]{3,2,1,0:T(8,128)(2,1)} reshape(bf16[1,2,32,32,384]{4,3,2,1,0:T(8,128)(2,1)S(1)} %get-tuple-element.4) | data formatting | bytes 3145728 | tf_op jit(solution)/shard_map/reshape;squeeze | solution.py:109
  275.0 3.4 %fusion.58 = (f32[2,6,32]{2,1,0:T(8,128)S(1)}, f32[2,6,32,1024]{3,2,1,0:T(8,128)S(1)}) fusion(bf16[2,1024,6,64]{3,2,1,0:T(8,128)(2,1)} %reshape_squeeze.18, bf16[2,32,6,64]{3,2,1,0:T(8,128)(2,1)S(1)} %reshape_squeeze.15, pred[2,1024]{1,0:T(4,128)(4,1)S(1)} %copy-done.7), kind=kOutput, calls=%fused_computation.86 | convolution fusion | flops 51510912 | bytes 3198464 | tf_op jit(solution)/shard_map/sqhd,skhd->shqk/dot_general | solution.py:112
  278.4 5.9 %reshape_squeeze.19 = bf16[2,1024,6,64]{3,2,1,0:T(8,128)(2,1)} reshape(bf16[1,2,32,32,384]{4,3,2,1,0:T(8,128)(2,1)} %get-tuple-element.5) | data formatting | bytes 3145728 | tf_op jit(solution)/shard_map/reshape;squeeze | solution.py:110
  284.3 0.4 fusion.8
  284.7 3.4 %fusion.16 = f32[2,32,6,64]{3,1,2,0:T(8,128)S(1)} fusion(bf16[2,1024,6,64]{3,2,1,0:T(8,128)(2,1)} %reshape_squeeze.19, f32[2,6,32,1024]{3,2,1,0:T(8,128)S(1)} %get-tuple-element.26, f32[2,6,32]{2,1,0:T(8,128)S(1)} %max.18), kind=kOutput, calls=%fused_computation.18 | convolution fusion | flops 51118080 | bytes 3245568 | tf_op jit(solution)/shard_map/shqk,skhd->shqd/dot_general | solution.py:123
  288.1 0.3 fusion.19
  288.6 0.1 convert_element_type.54
  288.7 0.7 copy-done.1
  289.4 1.2 convolution_convert_fusion
  291.3 34.3 %all-reduce.2.cloned.1.call-done = bf16[2,32,1536]{2,1,0:T(8,128)(2,1)} async-done(((bf16[2,32,1536]{2,1,0:T(8,128)(2,1)}), bf16[2,32,1536]{2,1,0:T(8,128)(2,1)}) %all-reduce.2.cloned.1.call-update) | async-done | bytes 196624 | tf_op jit(solution)/shard_map/psum | solution.py:146
  325.6 1.1 fusion.38
  326.7 1.1 multiply_reduce_fusion
  327.9 1.2 broadcast_multiply_fusion
  329.1 0.1 mul.213
  329.2 0.1 mul.214
  329.3 0.6 fusion.55
  (47 shorter events, 0.3 us)
Async XLA Ops:
  7.2 4.2 %copy-start = (f32[16,5,1536]{2,0,1:T(8,128)S(1)}, f32[16,5,1536]{2,0,1:T(8,128)}, u32[]{:S(2)}) copy-start(f32[16,5,1536]{2,0,1:T(8,128)} %param.16) | copy-start | bytes 1474564
  7.2 4.2 %copy-start.11 = (s32[2]{0:T(128)S(1)}, s32[2]{0:T(128)}, u32[]{:S(2)}) copy-start(s32[2]{0:T(128)} %param.14) | copy-start | bytes 28
  7.2 142.2 %all-gather.3.cloned.1.call-start = ((), (), s32[]{:S(2)}) async-start(), calls=%async_computation.1 | async-start | bytes 4737024 | tf_op jit(solution)/shard_map/all_gather | solution.py:81
  8.6 259.1 %all-gather.5.cloned.1.call-start = ((), (), s32[]{:S(2)}) async-start(), calls=%async_computation.2 | async-start | bytes 3244032 | tf_op jit(solution)/shard_map/all_gather | solution.py:104
  149.4 3.8 %copy-start.10 = (bf16[384,6]{0,1:T(8,128)(2,1)S(1)}, bf16[384,6]{0,1:T(8,128)(2,1)}, u32[]{:S(2)}) copy-start(bf16[384,6]{0,1:T(8,128)(2,1)} %param.20) | copy-start | bytes 13828
  154.4 11.4 %copy-start.12 = (s32[2]{0:T(128)S(1)}, s32[2]{0:T(128)}, u32[]{:S(2)}) copy-start(s32[2]{0:T(128)} %param.12) | copy-start | bytes 28
  154.4 11.4 %copy-start.13 = (s32[2]{0:T(128)S(1)}, s32[2]{0:T(128)}, u32[]{:S(2)}) copy-start(s32[2]{0:T(128)} %param.13) | copy-start | bytes 28
  154.4 12.8 %copy-start.2 = (bf16[2,2,154,384]{3,1,2,0:T(2,128)(2,1)S(1)}, bf16[2,2,154,384]{3,1,2,0:T(2,128)(2,1)}, u32[]{:S(2)}) copy-start(bf16[2,2,154,384]{3,1,2,0:T(2,128)(2,1)} %param.17) | copy-start | bytes 1419268
  154.4 55.3 %all-to-all-start = ((bf16[256,384,6]{1,2,0:T(8,128)(2,1)}), bf16[256,384,6]{1,2,0:T(8,128)(2,1)S(1)}, u32[]{:S(2)}, u32[]{:S(2)}) async-start(bf16[256,384,6]{1,2,0:T(8,128)(2,1)} %stack.2), calls=%async_computation | async-start | bytes 3145728 | tf_op jit(solution)/shard_map/all_to_all | solution.py:139
  165.6 160.1 %all-reduce.2.cloned.1.call-start = ((), (), s32[]{:S(2)}) async-start(), calls=%async_computation.3 | async-start | bytes 393216 | tf_op jit(solution)/shard_map/psum | solution.py:146
  171.8 39.3 %copy-start.3 = (bf16[2,1,154,384]{2,3,0,1:T(8,128)(2,1)S(1)}, bf16[2,1,154,384]{2,3,0,1:T(8,128)(2,1)}, u32[]{:S(2)}) copy-start(bf16[2,1,154,384]{2,3,0,1:T(8,128)(2,1)} %copy.38) | copy-start | bytes 709636
  271.3 3.7 %copy-start.7 = (pred[2,1024]{1,0:T(4,128)(4,1)S(1)}, pred[2,1024]{1,0:T(4,128)(4,1)}, u32[]{:S(2)}) copy-start(pred[2,1024]{1,0:T(4,128)(4,1)} %and.40) | copy-start | bytes 6148
  284.7 3.4 %copy-start.4 = (bf16[2,1,154,384]{2,3,0,1:T(8,128)(2,1)S(1)}, bf16[2,1,154,384]{2,3,0,1:T(8,128)(2,1)}, u32[]{:S(2)}) copy-start(bf16[2,1,154,384]{2,3,0,1:T(8,128)(2,1)} %copy.40) | copy-start | bytes 709636
  288.1 1.3 copy-start.1
  288.1 37.5 %copy-start.5 = (f32[2,1536]{1,0:T(2,128)S(1)}, f32[2,1536]{1,0:T(2,128)}, u32[]{:S(2)}) copy-start(f32[2,1536]{1,0:T(2,128)} %get-tuple-element.8) | copy-start | bytes 36868
  288.5 39.3 %copy-start.8 = (f32[2,1536]{1,0:T(2,128)S(1)}, f32[2,1536]{1,0:T(2,128)}, u32[]{:S(2)}) copy-start(f32[2,1536]{1,0:T(2,128)} %get-tuple-element.9) | copy-start | bytes 36868
  288.5 39.3 %copy-start.9 = (f32[2,1536]{1,0:T(2,128)S(1)}, f32[2,1536]{1,0:T(2,128)}, u32[]{:S(2)}) copy-start(f32[2,1536]{1,0:T(2,128)} %get-tuple-element.10) | copy-start | bytes 36868
  288.5 39.3 %copy-start.14 = (pred[2,32]{1,0:T(4,128)(4,1)S(1)}, pred[2,32]{1,0:T(4,128)(4,1)}, u32[]{:S(2)}) copy-start(pred[2,32]{1,0:T(4,128)(4,1)} %get-tuple-element.19) | copy-start | bytes 196
  288.5 39.3 %copy-start.15 = (bf16[1536,64]{0,1:T(8,128)(2,1)S(1)}, bf16[1536,64]{0,1:T(8,128)(2,1)}, u32[]{:S(2)}) copy-start(bf16[1536,64]{0,1:T(8,128)(2,1)} %param.21) | copy-start | bytes 589828
  290.5 38.7 %copy-start.6 = (f32[2,1,2048]{2,1,0:T(1,128)S(1)}, f32[2,1,2048]{2,1,0:T(1,128)}, u32[]{:S(2)}) copy-start(f32[2,1,2048]{2,1,0:T(1,128)} %param.11) | copy-start | bytes 49156
Sparse Core Ops, SparseCore 0:
  12.5 136.7 all-gather.2
  153.2 114.5 all-gather.4
  290.7 34.8 all-reduce.1
